TPU v7x, 256 devices: a whole 4x4x8 slice. The times are simulated.
256 devices in a mesh: dp: 8 (over x, core), graph: 32 (over y, z).
Axes of the slice: x: 4, y: 4, z: 8, core: 2. Of those that a mesh axis runs over, the one named last changes fastest.
Arguments:
- edges: bfloat16 [8, 65536, 1024], P('dp', 'graph'), may hold values from -6 to 6
- send_rows: int32 [8, 262144], P('dp', 'graph'), may hold values from 0 to 2047
- trip_src: int32 [8, 262144], P('dp', 'graph'), may hold values from 0 to 8191
- trip_dst: int32 [8, 262144], P('dp', 'graph'), may hold values from 0 to 2047
- basis_values: bfloat16 [8, 42, 262144], P('dp', None, 'graph'), may hold values from -6 to 6
- cotangent: bfloat16 [8, 65536, 1024], P('dp', 'graph'), may hold values from -6 to 6
- w_down: bfloat16 [1024, 128], replicated, may hold values from -0.1875 to 0.1875
- w_up: bfloat16 [128, 1024], replicated, may hold values from -0.5 to 0.5
- w_basis: bfloat16 [42, 128], replicated, may hold values from -1 to 1
Outputs:
- grad_edges: bfloat16 [8, 65536, 1024], P('dp', 'graph')
- grad_down: float32 [1024, 128], replicated
- grad_up: float32 [128, 1024], replicated
- grad_basis: float32 [42, 128], replicated
All inputs are finite; a program needn't handle non-finite values.
Results may differ from a plain program's by a relative error of at most 0.0073.
Values may be sent and summed in bfloat16 or wider, within the bound.
No kernel may reach another device: no remote copies, remote signals or barrier semaphores. Data moves between devices by JAX's collectives and lax.ppermute only.
A program may use at most 128 MiB of HBM per device.

v0:
```python
import jax
import jax.numpy as jnp
from jax import lax
from jax.sharding import PartitionSpec as P


def shards(edges, send_rows, trip_src, trip_dst, basis_values, cotangent, w_down, w_up, w_basis):
    edge_rows = edges[0]
    sendlist = send_rows[0]
    source_index = trip_src[0]
    target_index = trip_dst[0]
    basis_block = basis_values[0]
    grad_block = cotangent[0]
    local_edges = edge_rows.shape[0]
    down = jnp.dot(edge_rows, w_down, preferred_element_type=jnp.float32).astype(jnp.bfloat16)
    received = lax.all_to_all(
        jnp.take(down, sendlist, axis=0), "graph", split_axis=0, concat_axis=0, tiled=True
    )
    asked_rows = received.shape[0]
    source_rows = jnp.take(received, source_index, axis=0).astype(jnp.float32)
    basis_emb = lax.dot_general(
        basis_block, w_basis, (((0,), (0,)), ((), ())), preferred_element_type=jnp.float32
    )
    product = source_rows * basis_emb
    aggregate = jax.ops.segment_sum(product, target_index, num_segments=local_edges).astype(
        jnp.bfloat16
    )
    pre_act = jnp.dot(aggregate, w_up, preferred_element_type=jnp.float32)
    sigma = jax.nn.sigmoid(pre_act)
    g_pre = (grad_block.astype(jnp.float32) * sigma * (1.0 + pre_act * (1.0 - sigma))).astype(
        jnp.bfloat16
    )
    up_term = lax.dot_general(
        aggregate, g_pre, (((0,), (0,)), ((), ())), preferred_element_type=jnp.float32
    )
    g_agg = lax.dot_general(
        g_pre, w_up, (((1,), (1,)), ((), ())), preferred_element_type=jnp.float32
    )
    g_trip = jnp.take(g_agg, target_index, axis=0)
    g_source = g_trip * basis_emb
    g_basis_emb = g_trip * source_rows
    basis_term = jnp.dot(
        basis_block.astype(jnp.float32), g_basis_emb, precision=lax.Precision.HIGHEST
    )
    g_received = jax.ops.segment_sum(g_source, source_index, num_segments=asked_rows)
    returned = lax.all_to_all(g_received, "graph", split_axis=0, concat_axis=0, tiled=True)
    g_down = jax.ops.segment_sum(returned, sendlist, num_segments=local_edges).astype(jnp.bfloat16)
    grad_edges = lax.dot_general(
        g_down, w_down, (((1,), (1,)), ((), ())), preferred_element_type=jnp.float32
    )
    down_term = lax.dot_general(
        edge_rows, g_down, (((0,), (0,)), ((), ())), preferred_element_type=jnp.float32
    )
    grad_down, grad_up, grad_basis = lax.psum((down_term, up_term, basis_term), ("dp", "graph"))
    return (grad_edges.astype(jnp.bfloat16)[None], grad_down, grad_up, grad_basis)


def solution(mesh):
    in_specs = (
        P("dp", "graph", None),
        P("dp", "graph"),
        P("dp", "graph"),
        P("dp", "graph"),
        P("dp", None, "graph"),
        P("dp", "graph", None),
        P(),
        P(),
        P(),
    )
    out_specs = (P("dp", "graph", None), P(), P(), P())
    return jax.shard_map(shards, mesh=mesh, in_specs=in_specs, out_specs=out_specs, check_vma=False)
```

profile of v0, /device:TPU:2, one launch (start us, length us, event | category | flops | bytes accessed | tf_op | source)
XLA Modules:
  0.0 685.5 jit_solution(6888944162113069686)
XLA Ops:
  8.6 1.5 reduce.3
  10.1 3.5 fusion.12
  13.6 24.0 %gather_fusion = bf16[8192,128]{1,0:T(8,128)(2,1)S(1)} fusion(bf16[2048,128]{1,0:T(8,128)(2,1)S(1)} %fusion.12, s32[8192]{0:T(1024)S(1)} %broadcast_clamp_fusion.2), kind=kCustom, calls=%fused_computation | custom fusion | bytes 4227072 | tf_op jit(solution)/shard_map/jit(_take)/gather | solution.py:17
  37.7 2.7 broadcast_select_fusion.1
  40.3 11.5 %all-to-all-start = ((bf16[32,256,128]{2,1,0:T(8,128)(2,1)}), bf16[32,256,128]{2,1,0:T(8,128)(2,1)S(1)}, u32[]{:S(2)}, u32[]{:S(2)}) async-start(bf16[32,256,128]{2,1,0:T(8,128)(2,1)} %broadcast_select_fusion.1), calls=%async_computation | async-start | bytes 4194304 | tf_op jit(solution)/shard_map/all_to_all | solution.py:16
  52.0 2.8 fusion.25
  54.8 47.1 %all-to-all-done = bf16[32,256,128]{2,1,0:T(8,128)(2,1)S(1)} async-done(((bf16[32,256,128]{2,1,0:T(8,128)(2,1)}), bf16[32,256,128]{2,1,0:T(8,128)(2,1)S(1)}, u32[]{:S(2)}, u32[]{:S(2)}) %all-to-all-start) | async-done | bytes 2097184 | tf_op jit(solution)/shard_map/all_to_all | solution.py:16
  101.8 29.4 %gather_fusion.1 = bf16[8192,128]{1,0:T(8,128)(2,1)} fusion(bf16[8192,128]{1,0:T(8,128)(2,1)S(1)} %bitcast.46, s32[8192]{0:T(1024)S(1)} %broadcast_clamp_fusion), kind=kCustom, calls=%fused_computation.1 | custom fusion | bytes 4227072 | tf_op jit(solution)/shard_map/jit(_take)/gather | solution.py:20
  131.3 49.5 %scatter_custom_fusion = f32[2048,128]{1,0:T(8,128)S(1)} fusion(s32[8192]{0:T(1024)S(1)} %bitcast.50, f32[8192,128]{1,0:T(8,128)} %fusion.25, bf16[8192,128]{1,0:T(8,128)(2,1)} %gather_fusion.1, pred[8192]{0:T(1024)(128)(4,1)S(1)} %get-tuple-element.14, bf16[]{:T(256)} %constant.46.clone.1, f32[]{:T(128)} %constant.30.clone.1), kind=kCustom, calls=%fused_computation.11 | custom fusion | flops 4194304 | bytes 7348230 | tf_op jit(solution)/shard_map/scatter-add | solution.py:25
  180.8 5.7 fusion.1
  186.5 2.0 copy-done.1
  189.7 27.8 %gather_fusion.2 = f32[8192,128]{1,0:T(8,128)} fusion(f32[2048,128]{1,0:T(8,128)S(1)} %fusion.37, s32[8192]{0:T(1024)S(1)} %broadcast_clamp_fusion.1), kind=kCustom, calls=%fused_computation.2 | custom fusion | bytes 8421376 | tf_op jit(solution)/shard_map/jit(_take)/gather | solution.py:39
  217.5 51.4 %scatter_custom_fusion.1 = f32[8192,128]{1,0:T(8,128)} fusion(s32[8192]{0:T(1024)S(1)} %bitcast.52, f32[8192,128]{1,0:T(8,128)} %fusion.25, f32[8192,128]{1,0:T(8,128)} %gather_fusion.2, f32[]{:T(128)} %constant.47.clone.1, f32[]{:T(128)} %constant.30.clone.1, pred[8192]{0:T(1024)(128)(4,1)S(1)} %get-tuple-element.15), kind=kCustom, calls=%fused_computation.18 | custom fusion | flops 3145728 | bytes 12591112 | tf_op jit(solution)/shard_map/scatter-add | solution.py:45
  269.0 6.3 all-to-all-start.1
  275.3 3.7 fusion.32
  279.0 93.0 %all-to-all-done.1 = f32[32,256,128]{2,1,0:T(8,128)} async-done(((f32[32,256,128]{2,1,0:T(8,128)}), f32[32,256,128]{2,1,0:T(8,128)}, u32[]{:S(2)}, u32[]{:S(2)}) %all-to-all-start.1) | async-done | bytes 4194336 | tf_op jit(solution)/shard_map/all_to_all | solution.py:46
  372.0 45.4 %scatter_custom_fusion.2 = f32[2048,128]{1,0:T(8,128)} fusion(s32[8192]{0:T(1024)} %bitcast.53, f32[8192,128]{1,0:T(8,128)} %bitcast.15, f32[]{:T(128)} %constant.30.clone.1), kind=kCustom, calls=%fused_computation.35 | custom fusion | flops 1048576 | bytes 1049088 | tf_op jit(solution)/shard_map/scatter-add | solution.py:47
  417.4 4.0 fusion.20
  421.4 7.1 %fusion.23 = f32[42,128]{1,0:T(8,128)S(1)} fusion(f32[8192,128]{1,0:T(8,128)} %gather_fusion.2, pred[8192]{0:T(1024)(128)(4,1)S(1)} %get-tuple-element.15, bf16[8192,128]{1,0:T(8,128)(2,1)S(1)} %copy-done.2, pred[8192]{0:T(1024)(128)(4,1)S(1)} %get-tuple-element.14, bf16[1,42,8192]{2,1,0:T(8,128)(2,1)S(1)} %copy-done), kind=kOutput, calls=%fused_computation.31 | convolution fusion | flops 532676608 | bytes 7017472 | tf_op jit(solution)/shard_map/dot_general | solution.py:42
  428.5 74.3 %psum.23 = f32[42,128]{1,0:T(8,128)} all-reduce(f32[42,128]{1,0:T(8,128)S(1)} %fusion.23), channel_id=1, replica_groups=mesh['dp'=8,'graph'=32] {'dp','graph'}, use_global_device_ids=true, to_apply=%region_5.6 | all-reduce | flops 5376 | bytes 43008 | tf_op jit(solution)/shard_map/psum | solution.py:54
  502.8 4.5 convert_bitcast_fusion
  507.3 167.4 %all-reduce.3.cloned.1.call-done = (f32[1024,128]{0,1:T(8,128)}, f32[128,1024]{1,0:T(8,128)}) async-done(((f32[1024,128]{0,1:T(8,128)}, f32[128,1024]{1,0:T(8,128)}), (f32[1024,128]{0,1:T(8,128)}, f32[128,1024]{1,0:T(8,128)})) %all-reduce.3.cloned.1.call-update) | async-done | bytes 1048592 | tf_op jit(solution)/shard_map/psum | solution.py:54
  674.7 2.0 copy.14
  676.7 1.9 copy.17
  (28 shorter events, 2.9 us)
Async XLA Ops:
  7.2 44.8 %copy-start = (bf16[1,42,8192]{2,1,0:T(8,128)(2,1)S(1)}, bf16[1,42,8192]{2,1,0:T(8,128)(2,1)}, u32[]{:S(2)}) copy-start(bf16[1,42,8192]{2,1,0:T(8,128)(2,1)} %param.13) | copy-start | bytes 2064388
  37.6 14.2 %copy-start.6 = (s32[1,8192]{1,0:T(1,128)S(1)}, s32[1,8192]{1,0:T(1,128)}, u32[]{:S(2)}) copy-start(s32[1,8192]{1,0:T(1,128)} %param.11) | copy-start | bytes 98308
  37.6 14.3 %copy-start.5 = (s32[1,8192]{1,0:T(1,128)S(1)}, s32[1,8192]{1,0:T(1,128)}, u32[]{:S(2)}) copy-start(s32[1,8192]{1,0:T(1,128)} %param.12) | copy-start | bytes 98308
  37.6 14.4 %copy-start.7 = (bf16[42,128]{1,0:T(8,128)(2,1)S(1)}, bf16[42,128]{1,0:T(8,128)(2,1)}, u32[]{:S(2)}) copy-start(bf16[42,128]{1,0:T(8,128)(2,1)} %param.17) | copy-start | bytes 32260
  40.3 61.5 %all-to-all-start = ((bf16[32,256,128]{2,1,0:T(8,128)(2,1)}), bf16[32,256,128]{2,1,0:T(8,128)(2,1)S(1)}, u32[]{:S(2)}, u32[]{:S(2)}) async-start(bf16[32,256,128]{2,1,0:T(8,128)(2,1)} %broadcast_select_fusion.1), calls=%async_computation | async-start | bytes 4194304 | tf_op jit(solution)/shard_map/all_to_all | solution.py:16
  131.3 49.5 %copy-start.3 = (bf16[128,1024]{1,0:T(8,128)(2,1)S(1)}, bf16[128,1024]{1,0:T(8,128)(2,1)}, u32[]{:S(2)}) copy-start(bf16[128,1024]{1,0:T(8,128)(2,1)} %param.16) | copy-start | bytes 786436
  186.5 2.0 copy-start.1
  269.0 103.0 %all-to-all-start.1 = ((f32[32,256,128]{2,1,0:T(8,128)}), f32[32,256,128]{2,1,0:T(8,128)}, u32[]{:S(2)}, u32[]{:S(2)}) async-start(f32[32,256,128]{2,1,0:T(8,128)} %bitcast.47), calls=%async_computation.1 | async-start | bytes 8388608 | tf_op jit(solution)/shard_map/all_to_all | solution.py:46
  275.2 399.5 %all-reduce.3.cloned.1.call-start = ((), (), s32[]{:S(2)}) async-start(), calls=%async_computation.2 | async-start | bytes 2097152 | tf_op jit(solution)/shard_map/psum | solution.py:54
  279.0 142.4 %copy-start.2 = (bf16[8192,128]{1,0:T(8,128)(2,1)S(1)}, bf16[8192,128]{1,0:T(8,128)(2,1)}, u32[]{:S(2)}) copy-start(bf16[8192,128]{1,0:T(8,128)(2,1)} %gather_fusion.1) | copy-start | bytes 6291460
  421.4 81.4 %copy-start.4 = (bf16[1024,128]{1,0:T(8,128)(2,1)S(1)}, bf16[1024,128]{1,0:T(8,128)(2,1)}, u32[]{:S(2)}) copy-start(bf16[1024,128]{1,0:T(8,128)(2,1)} %param.15) | copy-start | bytes 786436
Sparse Core Ops, SparseCore 0:
  421.6 253.1 all-reduce.2
where the time goes:
time: 686 us; the launch traced here: 685 us
  waiting for transfers between devices  307 us (45%)
  other arithmetic  151 us (22%)
  local copies, waits for them, and re-layouts  87.8 us (13%)
  blocking collectives  74.3 us (11%)
  matrix products  32.5 us (5%)
  starting transfers between devices  17.8 us (3%)
  between operations  14.3 us (2%)
    psum x1, waiting for transfers between devices, shards(): lax.psum((down_term, up_term, basis_term), ('dp', 'graph'))  167 us
    all_to_all x1, waiting for transfers between devices, shards(): lax.all_to_all(g_received, 'graph', split_axis=0, concat_axis=0, tiled=True)  93 us
    psum x1, blocking collectives, shards(): lax.psum((down_term, up_term, basis_term), ('dp', 'graph'))  74.3 us
    scatter-add x1, other arithmetic, shards(): jax.ops.segment_sum(g_source, source_index, num_segments=asked_rows)  51.4 us
    scatter-add x1, other arithmetic, shards(): jax.ops.segment_sum(product, target_index, num_segments=local_edges)  49.5 us
    all_to_all x1, waiting for transfers between devices, shards(): lax.all_to_all(jnp.take(down, sendlist, axis=0), 'graph', split_axis=0, c...  47.1 us
    scatter-add x1, other arithmetic, shards(): jax.ops.segment_sum(returned, sendlist, num_segments=local_edges)  45.4 us
    gather x1, local copies, waits for them, and re-layouts, shards(): source_rows = jnp.take(received, source_index, axis=0).astype(jnp.float32)  29.4 us
  transfers between devices with their start and end apart: 3, of which 3 were waited for; matrix products, arithmetic and copies ran while one was open for 3% of the time, Pallas kernels for 0%

commit v1 on v0

--- a/solution.py
+++ b/solution.py
@@ -51,7 +51,9 @@
     down_term = lax.dot_general(
         edge_rows, g_down, (((0,), (0,)), ((), ())), preferred_element_type=jnp.float32
     )
-    grad_down, grad_up, grad_basis = lax.psum((down_term, up_term, basis_term), ("dp", "graph"))
+    grad_down, grad_up, grad_basis = lax.psum(
+        lax.psum((down_term, up_term, basis_term), "graph"), "dp"
+    )
     return (grad_edges.astype(jnp.bfloat16)[None], grad_down, grad_up, grad_basis)
 
 

time: 686 us -> 753 us (1.098)
  blocking collectives: 74.3 us -> 162 us
  waiting for transfers between devices: 307 us -> 286 us
    psum x1 -> x2, blocking collectives: 74.3 us -> 162 us  [the longest x1 140 us: shards(): lax.psum((down_term, up_term, basis_term), 'graph')]
    psum x1 -> x2, waiting for transfers between devices: 167 us -> 146 us  [the longest x1 146 us: shards(): lax.psum((down_term, up_term, basis_term), 'graph')]
  transfers between devices with their start and end apart: 3 -> 4, of which waited for: 3 -> 3; matrix products, arithmetic and copies ran while one was open for 3% -> 2% of each run, Pallas kernels for 0% -> 0%
where the time goes in v1:
time: 753 us; the launch traced here: 752 us
  waiting for transfers between devices  286 us (38%)
  blocking collectives  162 us (22%)
  other arithmetic  151 us (20%)
  local copies, waits for them, and re-layouts  87.4 us (12%)
  matrix products  32.6 us (4%)
  starting transfers between devices  17.8 us (2%)
  between operations  14.3 us (2%)
    psum x1, waiting for transfers between devices, shards(): lax.psum((down_term, up_term, basis_term), 'graph')  146 us
    psum x1, blocking collectives, shards(): lax.psum((down_term, up_term, basis_term), 'graph')  140 us
    all_to_all x1, waiting for transfers between devices, shards(): lax.all_to_all(g_received, 'graph', split_axis=0, concat_axis=0, tiled=True)  93 us
    scatter-add x1, other arithmetic, shards(): jax.ops.segment_sum(g_source, source_index, num_segments=asked_rows)  51.4 us
    scatter-add x1, other arithmetic, shards(): jax.ops.segment_sum(product, target_index, num_segments=local_edges)  49.5 us
    all_to_all x1, waiting for transfers between devices, shards(): lax.all_to_all(jnp.take(down, sendlist, axis=0), 'graph', split_axis=0, c...  47.1 us
    scatter-add x1, other arithmetic, shards(): jax.ops.segment_sum(returned, sendlist, num_segments=local_edges)  45.4 us
    gather x1, local copies, waits for them, and re-layouts, shards(): source_rows = jnp.take(received, source_index, axis=0).astype(jnp.float32)  29.2 us
  transfers between devices with their start and end apart: 4, of which 3 were waited for; matrix products, arithmetic and copies ran while one was open for 2% of the time, Pallas kernels for 0%

profile of v1, /device:TPU:2, one launch (start us, length us, event | category | flops | bytes accessed | tf_op | source)
XLA Modules:
  0.0 751.6 jit_solution(10304434281487639470)
XLA Ops:
  10.1 3.5 fusion.12
  13.6 24.0 %gather_fusion = bf16[8192,128]{1,0:T(8,128)(2,1)S(1)} fusion(bf16[2048,128]{1,0:T(8,128)(2,1)S(1)} %fusion.12, s32[8192]{0:T(1024)S(1)} %broadcast_clamp_fusion.2), kind=kCustom, calls=%fused_computation | custom fusion | bytes 4227072 | tf_op jit(solution)/shard_map/jit(_take)/gather | solution.py:17
  37.7 2.7 broadcast_select_fusion.1
  40.3 11.5 %all-to-all-start = ((bf16[32,256,128]{2,1,0:T(8,128)(2,1)}), bf16[32,256,128]{2,1,0:T(8,128)(2,1)S(1)}, u32[]{:S(2)}, u32[]{:S(2)}) async-start(bf16[32,256,128]{2,1,0:T(8,128)(2,1)} %broadcast_select_fusion.1), calls=%async_computation | async-start | bytes 4194304 | tf_op jit(solution)/shard_map/all_to_all | solution.py:16
  52.0 2.8 fusion.25
  54.8 47.1 %all-to-all-done = bf16[32,256,128]{2,1,0:T(8,128)(2,1)S(1)} async-done(((bf16[32,256,128]{2,1,0:T(8,128)(2,1)}), bf16[32,256,128]{2,1,0:T(8,128)(2,1)S(1)}, u32[]{:S(2)}, u32[]{:S(2)}) %all-to-all-start) | async-done | bytes 2097184 | tf_op jit(solution)/shard_map/all_to_all | solution.py:16
  101.9 29.2 %gather_fusion.1 = bf16[8192,128]{1,0:T(8,128)(2,1)} fusion(bf16[8192,128]{1,0:T(8,128)(2,1)S(1)} %bitcast.46, s32[8192]{0:T(1024)S(1)} %broadcast_clamp_fusion), kind=kCustom, calls=%fused_computation.1 | custom fusion | bytes 4227072 | tf_op jit(solution)/shard_map/jit(_take)/gather | solution.py:20
  131.1 49.5 %scatter_custom_fusion = f32[2048,128]{1,0:T(8,128)S(1)} fusion(s32[8192]{0:T(1024)S(1)} %bitcast.50, f32[8192,128]{1,0:T(8,128)} %fusion.25, bf16[8192,128]{1,0:T(8,128)(2,1)} %gather_fusion.1, pred[8192]{0:T(1024)(128)(4,1)S(1)} %get-tuple-element.16, bf16[]{:T(256)} %constant.46.clone.1, f32[]{:T(128)} %constant.30.clone.1), kind=kCustom, calls=%fused_computation.11 | custom fusion | flops 4194304 | bytes 7348230 | tf_op jit(solution)/shard_map/scatter-add | solution.py:25
  180.6 5.7 fusion.1
  186.3 2.0 copy-done.1
  189.5 27.7 %gather_fusion.2 = f32[8192,128]{1,0:T(8,128)} fusion(f32[2048,128]{1,0:T(8,128)S(1)} %fusion.37, s32[8192]{0:T(1024)S(1)} %broadcast_clamp_fusion.1), kind=kCustom, calls=%fused_computation.2 | custom fusion | bytes 8421376 | tf_op jit(solution)/shard_map/jit(_take)/gather | solution.py:39
  217.2 51.4 %scatter_custom_fusion.1 = f32[8192,128]{1,0:T(8,128)} fusion(s32[8192]{0:T(1024)S(1)} %bitcast.52, f32[8192,128]{1,0:T(8,128)} %fusion.25, f32[8192,128]{1,0:T(8,128)} %gather_fusion.2, f32[]{:T(128)} %constant.47.clone.1, f32[]{:T(128)} %constant.30.clone.1, pred[8192]{0:T(1024)(128)(4,1)S(1)} %get-tuple-element.17), kind=kCustom, calls=%fused_computation.18 | custom fusion | flops 3145728 | bytes 12591112 | tf_op jit(solution)/shard_map/scatter-add | solution.py:45
  268.6 6.3 all-to-all-start.1
  274.9 3.7 fusion.32
  278.7 93.0 %all-to-all-done.1 = f32[32,256,128]{2,1,0:T(8,128)} async-done(((f32[32,256,128]{2,1,0:T(8,128)}), f32[32,256,128]{2,1,0:T(8,128)}, u32[]{:S(2)}, u32[]{:S(2)}) %all-to-all-start.1) | async-done | bytes 4194336 | tf_op jit(solution)/shard_map/all_to_all | solution.py:46
  371.6 45.4 %scatter_custom_fusion.2 = f32[2048,128]{1,0:T(8,128)} fusion(s32[8192]{0:T(1024)} %bitcast.53, f32[8192,128]{1,0:T(8,128)} %bitcast.15, f32[]{:T(128)} %constant.30.clone.1), kind=kCustom, calls=%fused_computation.35 | custom fusion | flops 1048576 | bytes 1049088 | tf_op jit(solution)/shard_map/scatter-add | solution.py:47
  417.0 4.2 fusion.20
  421.3 146.2 %all-reduce.5.cloned.1.call-done = (f32[1024,128]{0,1:T(8,128)}, f32[128,1024]{1,0:T(8,128)}) async-done(((f32[1024,128]{0,1:T(8,128)}, f32[128,1024]{1,0:T(8,128)}), (f32[1024,128]{0,1:T(8,128)}, f32[128,1024]{1,0:T(8,128)})) %all-reduce.5.cloned.1.call-update) | async-done | bytes 1048592 | tf_op jit(solution)/shard_map/psum | solution.py:55
  567.6 7.0 fusion.23
  574.6 140.4 %psum.46 = f32[42,128]{1,0:T(8,128)S(1)} all-reduce(f32[42,128]{1,0:T(8,128)S(1)} %fusion.23), channel_id=1, replica_groups=mesh['dp'=8,'graph'=32] {'graph'}, use_global_device_ids=true, to_apply=%region_7.8 | all-reduce | flops 5376 | bytes 43008 | tf_op jit(solution)/shard_map/psum | solution.py:55
  715.0 21.3 %psum.47 = f32[42,128]{1,0:T(8,128)} all-reduce(f32[42,128]{1,0:T(8,128)S(1)} %psum.46), channel_id=1, replica_groups=mesh['dp'=8,'graph'=32] {'dp'}, use_global_device_ids=true, to_apply=%region_8.9 | all-reduce | flops 5376 | bytes 43008 | tf_op jit(solution)/shard_map/psum | solution.py:54
  736.3 4.5 convert_bitcast_fusion
  740.8 2.0 copy.14
  742.8 1.9 copy.19
  (32 shorter events, 4.4 us)
Async XLA Ops:
  7.2 44.8 %copy-start = (bf16[1,42,8192]{2,1,0:T(8,128)(2,1)S(1)}, bf16[1,42,8192]{2,1,0:T(8,128)(2,1)}, u32[]{:S(2)}) copy-start(bf16[1,42,8192]{2,1,0:T(8,128)(2,1)} %param.13) | copy-start | bytes 2064388
  37.6 14.2 %copy-start.6 = (s32[1,8192]{1,0:T(1,128)S(1)}, s32[1,8192]{1,0:T(1,128)}, u32[]{:S(2)}) copy-start(s32[1,8192]{1,0:T(1,128)} %param.11) | copy-start | bytes 98308
  37.6 14.3 %copy-start.5 = (s32[1,8192]{1,0:T(1,128)S(1)}, s32[1,8192]{1,0:T(1,128)}, u32[]{:S(2)}) copy-start(s32[1,8192]{1,0:T(1,128)} %param.12) | copy-start | bytes 98308
  37.6 14.4 %copy-start.7 = (bf16[42,128]{1,0:T(8,128)(2,1)S(1)}, bf16[42,128]{1,0:T(8,128)(2,1)}, u32[]{:S(2)}) copy-start(bf16[42,128]{1,0:T(8,128)(2,1)} %param.17) | copy-start | bytes 32260
  40.3 61.5 %all-to-all-start = ((bf16[32,256,128]{2,1,0:T(8,128)(2,1)}), bf16[32,256,128]{2,1,0:T(8,128)(2,1)S(1)}, u32[]{:S(2)}, u32[]{:S(2)}) async-start(bf16[32,256,128]{2,1,0:T(8,128)(2,1)} %broadcast_select_fusion.1), calls=%async_computation | async-start | bytes 4194304 | tf_op jit(solution)/shard_map/all_to_all | solution.py:16
  131.1 49.5 %copy-start.3 = (bf16[128,1024]{1,0:T(8,128)(2,1)S(1)}, bf16[128,1024]{1,0:T(8,128)(2,1)}, u32[]{:S(2)}) copy-start(bf16[128,1024]{1,0:T(8,128)(2,1)} %param.16) | copy-start | bytes 786436
  186.3 2.0 copy-start.1
  268.6 103.0 %all-to-all-start.1 = ((f32[32,256,128]{2,1,0:T(8,128)}), f32[32,256,128]{2,1,0:T(8,128)}, u32[]{:S(2)}, u32[]{:S(2)}) async-start(f32[32,256,128]{2,1,0:T(8,128)} %bitcast.47), calls=%async_computation.1 | async-start | bytes 8388608 | tf_op jit(solution)/shard_map/all_to_all | solution.py:46
  274.9 292.6 %all-reduce.5.cloned.1.call-start = ((), (), s32[]{:S(2)}) async-start(), calls=%async_computation.2 | async-start | bytes 2097152 | tf_op jit(solution)/shard_map/psum | solution.py:55
  417.0 150.6 %copy-start.2 = (bf16[8192,128]{1,0:T(8,128)(2,1)S(1)}, bf16[8192,128]{1,0:T(8,128)(2,1)}, u32[]{:S(2)}) copy-start(bf16[8192,128]{1,0:T(8,128)(2,1)} %gather_fusion.1) | copy-start | bytes 6291460
  421.2 315.1 %copy-start.4 = (bf16[1024,128]{1,0:T(8,128)(2,1)S(1)}, bf16[1024,128]{1,0:T(8,128)(2,1)}, u32[]{:S(2)}) copy-start(bf16[1024,128]{1,0:T(8,128)(2,1)} %param.15) | copy-start | bytes 786436
  421.2 319.5 %all-reduce.7.cloned.1.call-start = ((), (), s32[]{:S(2)}) async-start(), calls=%async_computation.3 | async-start | bytes 2097152 | tf_op jit(solution)/shard_map/psum | solution.py:54
Sparse Core Ops, SparseCore 0:
  421.4 146.1 all-reduce.4
  570.0 62.9 all-reduce.6
